TPU v7x, 512 devices: a whole 4x4x16 slice. The times are simulated.
512 devices in a mesh: dp: 16 (over z), pipe: 4 (over x), tensor: 8 (over y, core).
Axes of the slice: x: 4, y: 4, z: 16, core: 2. Of those that a mesh axis runs over, the one named last changes fastest.
Arguments:
- tokens: bfloat16 [16384, 8192], P('dp', ('pipe', 'tensor')), may hold values from -6 to 6
- key_value_weight: bfloat16 [8192, 2048], P(('pipe', 'tensor')), may hold values from -0.0625 to 0.0625
- adapter_down: bfloat16 [96, 8192, 128], P(None, ('pipe', 'tensor', 'dp')), may hold values from -0.0625 to 0.0625
- adapter_up: bfloat16 [96, 64, 2048], P(None, 'dp'), may hold values from -0.75 to 0.75
- tenant_of_block: int32 [128], replicated, may hold values from 0 to 95
- slot_of_tenant: int32 [96], replicated, may hold values from 0 to 95, each once
- cotangent: bfloat16 [16384, 2048], P(('dp', 'pipe', 'tensor')), may hold values from -1.5 to 1.5
Outputs:
- key_value: bfloat16 [16384, 2048], P(('dp', 'pipe', 'tensor'))
- input_grad: bfloat16 [16384, 8192], P('dp', ('pipe', 'tensor'))
- grad_a: float32 [96, 8192, 128], P(None, ('pipe', 'tensor', 'dp'))
- grad_b: float32 [96, 64, 2048], P(None, 'dp', ('pipe', 'tensor'))
Inputs may be any that keep to these rules, and one draw needn't show every extreme that they name: `slot_of_tenant`: each slot holds exactly one tenant.
All inputs are finite; a program needn't handle non-finite values.
Results may differ from a plain program's by a relative error of at most 0.017.
Values may be sent and summed in bfloat16 or wider, within the bound.
A program may use at most 64 MiB of HBM per device.

v0:
```python
import jax
import jax.numpy as jnp
from jax import lax
from jax.sharding import PartitionSpec as P

KEY_WIDTH = 1024
ADAPTER_RANK = 64
BLOCK = 128


def body(
    tokens, key_value_weight, adapter_down, adapter_up, tenant_of_block, slot_of_tenant, cotangent
):
    data_count = lax.axis_size("dp")
    group_count = lax.axis_size(("pipe", "tensor"))
    my_group = lax.axis_index(("pipe", "tensor"))
    tok_dev, feature_count = tokens.shape
    blocks_dev = tok_dev // BLOCK
    row_count = tok_dev // group_count
    tenant_list = slot_of_tenant.shape[0]
    all_blocks = tenant_of_block.shape[0]
    tenant_ids = lax.broadcasted_iota(jnp.int32, (all_blocks, tenant_list), 1)
    slot_of_block = jnp.sum(
        jnp.where(tenant_of_block[:, None] == tenant_ids, slot_of_tenant[None, :], 0), axis=1
    )
    slot_match = slot_of_block[:, None] == tenant_ids
    down_rows = adapter_down.shape[1]
    a_send = jnp.dot(
        slot_match.astype(jnp.bfloat16),
        adapter_down.reshape(tenant_list, down_rows * 2 * ADAPTER_RANK),
        preferred_element_type=jnp.float32,
    )
    a_send = a_send.astype(jnp.bfloat16).reshape(all_blocks, down_rows, 2 * ADAPTER_RANK)
    own_block = my_group * row_count // BLOCK
    own_slots = lax.dynamic_index_in_dim(
        slot_of_block.reshape(data_count, blocks_dev), own_block, 1, False
    )
    owner_choice = (
        own_slots[:, None] == lax.broadcasted_iota(jnp.int32, (data_count, tenant_list), 1)
    ).astype(jnp.bfloat16)
    up_rows = adapter_up.shape[1]
    b_send = jnp.dot(
        owner_choice,
        adapter_up.reshape(tenant_list, up_rows * 2 * KEY_WIDTH),
        preferred_element_type=jnp.float32,
    )
    b_send = b_send.astype(jnp.bfloat16).reshape(data_count, up_rows, 2 * KEY_WIDTH)
    down_blocks, b_own = (
        lax.all_to_all(a_send, "dp", split_axis=0, concat_axis=1, tiled=True),
        lax.all_to_all(b_send, "dp", split_axis=0, concat_axis=1, tiled=True),
    )
    b_own = b_own[0]
    tok_blocks = tokens.reshape(blocks_dev, BLOCK, feature_count)
    low_part = jnp.einsum(
        "bif,bfr->bir", tok_blocks, down_blocks, preferred_element_type=jnp.float32
    ).reshape(tok_dev, 2 * ADAPTER_RANK)
    low_all = lax.psum(low_part.astype(jnp.bfloat16), ("pipe", "tensor"))
    base_out = lax.psum_scatter(
        jnp.dot(tokens, key_value_weight, preferred_element_type=jnp.float32).astype(jnp.bfloat16),
        ("pipe", "tensor"),
        scatter_dimension=0,
        tiled=True,
    ).astype(jnp.float32)
    low_rows = lax.dynamic_slice_in_dim(low_all, my_group * row_count, row_count, 0)
    lowrank = jnp.concatenate(
        [
            jnp.dot(
                low_rows[:, :ADAPTER_RANK], b_own[:, :KEY_WIDTH], preferred_element_type=jnp.float32
            ),
            jnp.dot(
                low_rows[:, ADAPTER_RANK:], b_own[:, KEY_WIDTH:], preferred_element_type=jnp.float32
            ),
        ],
        axis=1,
    )
    key_value = (base_out + lowrank).astype(jnp.bfloat16)
    contract_last = (((1,), (1,)), ((), ()))
    grad_rows = jnp.concatenate(
        [
            lax.dot_general(
                cotangent[:, :KEY_WIDTH],
                b_own[:, :KEY_WIDTH],
                contract_last,
                preferred_element_type=jnp.float32,
            ),
            lax.dot_general(
                cotangent[:, KEY_WIDTH:],
                b_own[:, KEY_WIDTH:],
                contract_last,
                preferred_element_type=jnp.float32,
            ),
        ],
        axis=1,
    )
    grad_rows = grad_rows.astype(jnp.bfloat16)
    cot_all, grad_low = (
        lax.all_gather(cotangent, ("pipe", "tensor"), axis=0, tiled=True),
        lax.all_gather(grad_rows, ("pipe", "tensor"), axis=0, tiled=True),
    )
    grad_blocks = grad_low.reshape(blocks_dev, BLOCK, 2 * ADAPTER_RANK)
    input_grad = lax.dot_general(
        cot_all, key_value_weight, contract_last, preferred_element_type=jnp.float32
    )
    input_grad = input_grad + jnp.einsum(
        "bir,bfr->bif", grad_blocks, down_blocks, preferred_element_type=jnp.float32
    ).reshape(tok_dev, feature_count)
    input_grad = input_grad.astype(jnp.bfloat16)
    grad_a_part = jnp.einsum(
        "bif,bir->bfr", tok_blocks, grad_blocks, preferred_element_type=jnp.float32
    )
    col_count = 2 * KEY_WIDTH // group_count
    col_start = my_group * col_count
    half_index = col_start // KEY_WIDTH
    low_half = lax.dynamic_slice_in_dim(
        low_all, half_index * ADAPTER_RANK, ADAPTER_RANK, 1
    ).reshape(blocks_dev, BLOCK, ADAPTER_RANK)
    cot_cols = lax.dynamic_slice_in_dim(cot_all, col_start, col_count, 1).reshape(
        blocks_dev, BLOCK, col_count
    )
    grad_b_part = jnp.einsum("bir,bic->brc", low_half, cot_cols, preferred_element_type=jnp.float32)
    grad_a_recv, grad_b_recv = (
        lax.all_to_all(
            grad_a_part.astype(jnp.bfloat16), "dp", split_axis=1, concat_axis=0, tiled=True
        ).astype(grad_a_part.dtype),
        lax.all_to_all(
            grad_b_part.astype(jnp.bfloat16), "dp", split_axis=1, concat_axis=0, tiled=True
        ).astype(grad_b_part.dtype),
    )
    slot_weight = slot_match.astype(jnp.float32)
    grad_a = jnp.einsum(
        "bt,bx->tx",
        slot_weight,
        grad_a_recv.reshape(all_blocks, down_rows * 2 * ADAPTER_RANK),
        precision=lax.Precision.HIGHEST,
    )
    grad_a = grad_a.reshape(tenant_list, down_rows, 2 * ADAPTER_RANK)
    grad_b = jnp.einsum(
        "bt,bx->tx",
        slot_weight,
        grad_b_recv.reshape(all_blocks, grad_b_recv.shape[1] * col_count),
        precision=lax.Precision.HIGHEST,
    )
    grad_b = grad_b.reshape(tenant_list, grad_b_recv.shape[1], col_count)
    return (key_value, input_grad, grad_a, grad_b)


def solution(mesh):
    placed = (
        P("dp", ("pipe", "tensor")),
        P(("pipe", "tensor"), None),
        P(None, ("pipe", "tensor", "dp"), None),
        P(None, "dp", None),
        P(),
        P(),
        P(("dp", "pipe", "tensor"), None),
    )
    return jax.shard_map(
        body,
        mesh=mesh,
        in_specs=placed,
        out_specs=(
            P(("dp", "pipe", "tensor"), None),
            P("dp", ("pipe", "tensor")),
            P(None, ("pipe", "tensor", "dp"), None),
            P(None, "dp", ("pipe", "tensor")),
        ),
        check_vma=False,
    )
```

profile of v0, /device:TPU:2, one launch (start us, length us, event | category | flops | bytes accessed | tf_op | source)
XLA Modules:
  0.0 395.1 jit_solution(17106891758424243477)
XLA Ops:
  7.2 0.9 select_reduce_fusion
  8.1 1.3 fusion.2
  9.6 44.1 %all_to_all.57 = bf16[128,16,128]{2,1,0:T(8,128)(2,1)S(1)} all-to-all(bf16[128,16,128]{2,1,0:T(8,128)(2,1)S(1)} %bitcast.78), channel_id=1, replica_groups=mesh['dp'=16,'pipe'=4,'tensor'=8] {'dp'}, dimensions={0} | all-to-all | bytes 1048576 | tf_op jit(solution)/shard_map/all_to_all | solution.py:49
  53.7 0.8 copy-done.2
  54.5 0.3 convolution_convert_fusion.4
  54.8 0.9 copy.41
  55.7 3.2 convolution_convert_fusion.1
  59.1 0.7 all-gather.2.cloned.1.call-update
  59.8 2.4 copy.61
  62.5 0.4 convolution_convert_fusion
  63.0 24.5 %all_to_all.58 = bf16[16,4,2048]{2,1,0:T(4,128)(2,1)S(1)} all-to-all(bf16[16,4,2048]{2,1,0:T(4,128)(2,1)S(1)} %reshape.64), channel_id=1, replica_groups=mesh['dp'=16,'pipe'=4,'tensor'=8] {'dp'}, dimensions={0} | all-to-all | bytes 524288 | tf_op jit(solution)/shard_map/all_to_all | solution.py:50
  87.9 0.4 copy-done.4
  88.4 24.9 %all_gather.7 = bf16[1024,128]{1,0:T(8,128)(2,1)S(1)} all-gather(bf16[32,128]{1,0:T(8,128)(2,1)S(1)} %pad_maximum_fusion), channel_id=1, replica_groups=mesh['dp'=16,'pipe'=4,'tensor'=8] {'pipe','tensor'}, dimensions={0}, use_global_device_ids=true | all-gather | bytes 270336 | tf_op jit(solution)/shard_map/all_gather | solution.py:98
  113.3 0.3 fusion.1
  113.6 1.1 copy.43
  114.7 5.8 %all-to-all-start.2 = ((bf16[8,256,128]{2,0,1:T(8,128)(2,1)}), bf16[8,256,128]{2,0,1:T(8,128)(2,1)S(1)}, u32[]{:S(2)}, u32[]{:S(2)}) async-start(bf16[8,256,128]{2,0,1:T(8,128)(2,1)} %copy.43), calls=%async_computation.3 | async-start | bytes 1048576 | tf_op jit(solution)/shard_map/all_to_all | solution.py:122
  120.5 0.3 fusion.30
  120.8 63.9 %all-reduce.2.cloned.1.call-done = bf16[1024,128]{0,1:T(8,128)(2,1)} async-done(((bf16[1024,128]{0,1:T(8,128)(2,1)}), bf16[1024,128]{0,1:T(8,128)(2,1)}) %all-reduce.2.cloned.1.call-update) | async-done | bytes 262160 | tf_op jit(solution)/shard_map/psum | solution.py:57
  184.8 1.2 fusion.14
  185.9 1.2 fusion.11
  187.4 0.3 fusion.21
  187.7 1.3 copy.53
  189.1 105.7 %reduce-scatter.2.cloned.1.call-done = bf16[32,2048]{1,0:T(8,128)(2,1)} async-done(((bf16[1024,2048]{1,0:T(8,128)(2,1)}), bf16[32,2048]{1,0:T(8,128)(2,1)}) %reduce-scatter.2.cloned.1.call-update) | async-done | bytes 131088 | tf_op jit(solution)/shard_map/reduce_scatter | solution.py:58
  294.8 1.6 fusion.7
  296.4 62.4 %all-gather.2.cloned.1.call-done = bf16[1024,2048]{1,0:T(8,128)(2,1)} async-done(((bf16[32,2048]{1,0:T(8,128)(2,1)}), bf16[1024,2048]{1,0:T(8,128)(2,1)}) %all-gather.2.cloned.1.call-update) | async-done | bytes 4194320 | tf_op jit(solution)/shard_map/all_gather | solution.py:97
  358.8 1.1 constant_dynamic-slice_fusion
  359.9 1.1 convolution_convert_fusion.5
  361.1 0.8 reshape.73
  361.9 12.3 %all-to-all-start.3 = ((bf16[16,2,1024]{2,1,0:T(2,128)(2,1)}), bf16[16,2,1024]{2,1,0:T(2,128)(2,1)S(1)}, u32[]{:S(2)}, u32[]{:S(2)}) async-start(bf16[16,2,1024]{2,1,0:T(2,128)(2,1)} %reshape.73), calls=%async_computation.4 | async-start | bytes 131072 | tf_op jit(solution)/shard_map/all_to_all | solution.py:125
  374.2 4.3 %fusion = bf16[1024,256]{1,0:T(8,128)(2,1)} fusion(f32[1024,256]{1,0:T(8,128)S(1)} %bitcast.81, bf16[1024,2048]{1,0:T(8,128)(2,1)} %all-gather.2.cloned.1.call-done, bf16[256,2048]{1,0:T(8,128)(2,1)S(1)} %copy-done), kind=kOutput, calls=%fused_computation.4 | convolution fusion | flops 1074266112 | bytes 6815744 | tf_op jit(solution)/shard_map/dot_general | solution.py:101
  378.4 8.9 %all-to-all-done.3 = bf16[16,2,1024]{2,1,0:T(2,128)(2,1)S(1)} async-done(((bf16[16,2,1024]{2,1,0:T(2,128)(2,1)}), bf16[16,2,1024]{2,1,0:T(2,128)(2,1)S(1)}, u32[]{:S(2)}, u32[]{:S(2)}) %all-to-all-start.3) | async-done | bytes 65568 | tf_op jit(solution)/shard_map/all_to_all | solution.py:125
  387.8 0.8 fusion.19
  (31 shorter events, 2.0 us)
Async XLA Ops:
  7.2 48.6 %copy-start = (bf16[256,2048]{1,0:T(8,128)(2,1)S(1)}, bf16[256,2048]{1,0:T(8,128)(2,1)}, u32[]{:S(2)}) copy-start(bf16[256,2048]{1,0:T(8,128)(2,1)} %param.8) | copy-start | bytes 3145732
  7.2 47.3 %copy-start.1 = (bf16[1024,256]{1,0:T(8,128)(2,1)S(1)}, bf16[1024,256]{1,0:T(8,128)(2,1)}, u32[]{:S(2)}) copy-start(bf16[1024,256]{1,0:T(8,128)(2,1)} %param.7) | copy-start | bytes 1572868
  7.2 177.6 %all-reduce.2.cloned.1.call-start = ((), (), s32[]{:S(2)}) async-start(), calls=%async_computation.6 | async-start | bytes 524288 | tf_op jit(solution)/shard_map/psum | solution.py:57
  53.7 0.8 copy-start.2
  55.7 239.1 %reduce-scatter.2.cloned.1.call-start = ((), (), s32[]{:S(2)}) async-start(), calls=%async_computation.5 | async-start | bytes 4325376 | tf_op jit(solution)/shard_map/reduce_scatter | solution.py:58
  59.0 28.6 %copy-start.5 = (bf16[32,2048]{1,0:T(8,128)(2,1)S(1)}, bf16[32,2048]{1,0:T(8,128)(2,1)}, u32[]{:S(2)}) copy-start(bf16[32,2048]{1,0:T(8,128)(2,1)} %param.13) | copy-start | bytes 393220
  59.0 299.8 %all-gather.2.cloned.1.call-start = ((), (), s32[]{:S(2)}) async-start(), calls=%async_computation.7 | async-start | bytes 4325376 | tf_op jit(solution)/shard_map/all_gather | solution.py:97
  62.8 57.7 %copy-start.3 = (bf16[16,8,16,128]{3,2,0,1:T(8,128)(2,1)S(1)}, bf16[16,8,16,128]{3,2,0,1:T(8,128)(2,1)}, u32[]{:S(2)}) copy-start(bf16[16,8,16,128]{3,2,0,1:T(8,128)(2,1)} %copy-done.2) | copy-start | bytes 1572868
  87.6 0.7 copy-start.4
  114.7 72.4 %all-to-all-start.2 = ((bf16[8,256,128]{2,0,1:T(8,128)(2,1)}), bf16[8,256,128]{2,0,1:T(8,128)(2,1)S(1)}, u32[]{:S(2)}, u32[]{:S(2)}) async-start(bf16[8,256,128]{2,0,1:T(8,128)(2,1)} %copy.43), calls=%async_computation.3 | async-start | bytes 1048576 | tf_op jit(solution)/shard_map/all_to_all | solution.py:122
  361.9 25.5 %all-to-all-start.3 = ((bf16[16,2,1024]{2,1,0:T(2,128)(2,1)}), bf16[16,2,1024]{2,1,0:T(2,128)(2,1)S(1)}, u32[]{:S(2)}, u32[]{:S(2)}) async-start(bf16[16,2,1024]{2,1,0:T(2,128)(2,1)} %reshape.73), calls=%async_computation.4 | async-start | bytes 131072 | tf_op jit(solution)/shard_map/all_to_all | solution.py:125
Sparse Core Ops, SparseCore 0:
  55.8 128.9 all-reduce.1
  189.3 105.4 reduce-scatter.1
  297.9 60.8 all-gather.1
where the time goes:
time: 396 us; the launch traced here: 395 us
  waiting for transfers between devices  242 us (61%)
  blocking collectives  93.4 us (24%)
  starting transfers between devices  18.2 us (5%)
  matrix products  15 us (4%)
  between operations  14 us (4%)
  local copies, waits for them, and re-layouts  10.2 us (3%)
    reduce_scatter x1, waiting for transfers between devices, body(): lax.psum_scatter(jnp.dot(tokens, key_value_weight, preferred_element_type...  106 us
    psum x1, waiting for transfers between devices, body(): low_all = lax.psum(low_part.astype(jnp.bfloat16), ('pipe', 'tensor'))  63.9 us
    all_gather x1, waiting for transfers between devices, body(): lax.all_gather(cotangent, ('pipe', 'tensor'), axis=0, tiled=True)  62.4 us
    all_to_all x1, blocking collectives, body(): lax.all_to_all(a_send, 'dp', split_axis=0, concat_axis=1, tiled=True)  44.1 us
    all_gather x1, blocking collectives, body(): lax.all_gather(grad_rows, ('pipe', 'tensor'), axis=0, tiled=True)  24.9 us
    all_to_all x1, blocking collectives, body(): lax.all_to_all(b_send, 'dp', split_axis=0, concat_axis=1, tiled=True)  24.5 us
    all_to_all x1, starting transfers between devices, body(): lax.all_to_all(grad_b_part.astype(jnp.bfloat16), 'dp', split_axis=1, conc...  12.3 us
    all_to_all x1, waiting for transfers between devices, body(): lax.all_to_all(grad_b_part.astype(jnp.bfloat16), 'dp', split_axis=1, conc...  8.89 us
  transfers between devices with their start and end apart: 5, of which 4 were waited for; matrix products, arithmetic and copies ran while one was open for 5% of the time, Pallas kernels for 0%

commit v1 on v0

--- a/solution.py
+++ b/solution.py
@@ -54,7 +54,7 @@
     low_part = jnp.einsum(
         "bif,bfr->bir", tok_blocks, down_blocks, preferred_element_type=jnp.float32
     ).reshape(tok_dev, 2 * ADAPTER_RANK)
-    low_all = lax.psum(low_part.astype(jnp.bfloat16), ("pipe", "tensor"))
+    low_all = jnp.sum(lax.all_gather(low_part.astype(jnp.bfloat16), ("pipe", "tensor")), axis=0)
     base_out = lax.psum_scatter(
         jnp.dot(tokens, key_value_weight, preferred_element_type=jnp.float32).astype(jnp.bfloat16),
         ("pipe", "tensor"),

time: 396 us -> 267 us (0.67)
  waiting for transfers between devices: 242 us -> 117 us
  starting transfers between devices: 18.2 us -> 12.5 us
  other arithmetic: 2.55 us -> 7.22 us
    psum x1 -> x0, waiting for transfers between devices: 63.9 us -> none  [body(): low_all = lax.psum(low_part.astype(jnp.bfloat16), ('pipe', 'tensor'))]
    all_gather x1, waiting for transfers between devices: 62.4 us -> 0.01 us  [body(): lax.all_gather(cotangent, ('pipe', 'tensor'), axis=0, tiled=True)]
    all_to_all x1, waiting for transfers between devices: 0.01 us -> 29 us  [body(): lax.all_to_all(grad_a_part.astype(jnp.bfloat16), 'dp', split_axis=1, conc...]
    reduce_scatter x1, waiting for transfers between devices: 106 us -> 87.5 us  [body(): lax.psum_scatter(jnp.dot(tokens, key_value_weight, preferred_element_type...]
    all_to_all x1, waiting for transfers between devices: 8.89 us -> 0.01 us  [body(): lax.all_to_all(grad_b_part.astype(jnp.bfloat16), 'dp', split_axis=1, conc...]
    all_to_all x1, starting transfers between devices: 12.3 us -> 6.58 us  [body(): lax.all_to_all(grad_b_part.astype(jnp.bfloat16), 'dp', split_axis=1, conc...]
    reduce_sum x0 -> x1, other arithmetic: none -> 4.79 us  [body(): jnp.sum(lax.all_gather(low_part.astype(jnp.bfloat16), ('pipe', 'tensor'))...]
  transfers between devices with their start and end apart: 5 -> 5, of which waited for: 4 -> 2; matrix products, arithmetic and copies ran while one was open for 5% -> 10% of each run, Pallas kernels for 0% -> 0%
where the time goes in v1:
time: 267 us
  waiting for transfers between devices  117 us (44%)
  blocking collectives  93.4 us (35%)
  between operations  14 us (5%)
  matrix products  12.9 us (5%)
  starting transfers between devices  12.5 us (5%)
  local copies, waits for them, and re-layouts  9.53 us (4%)
  other arithmetic  7.22 us (3%)
    reduce_scatter x1, waiting for transfers between devices, body(): lax.psum_scatter(jnp.dot(tokens, key_value_weight, preferred_element_type...  87.5 us
    all_to_all x1, blocking collectives, body(): lax.all_to_all(a_send, 'dp', split_axis=0, concat_axis=1, tiled=True)  44.1 us
    all_to_all x1, waiting for transfers between devices, body(): lax.all_to_all(grad_a_part.astype(jnp.bfloat16), 'dp', split_axis=1, conc...  29 us
    all_gather x1, blocking collectives, body(): lax.all_gather(grad_rows, ('pipe', 'tensor'), axis=0, tiled=True)  24.9 us
    all_to_all x1, blocking collectives, body(): lax.all_to_all(b_send, 'dp', split_axis=0, concat_axis=1, tiled=True)  24.5 us
    all_to_all x1, starting transfers between devices, body(): lax.all_to_all(grad_b_part.astype(jnp.bfloat16), 'dp', split_axis=1, conc...  6.58 us
    unnamed x19, local copies, waits for them, and re-layouts  6.01 us
    all_to_all x1, starting transfers between devices, body(): lax.all_to_all(grad_a_part.astype(jnp.bfloat16), 'dp', split_axis=1, conc...  5.81 us
  transfers between devices with their start and end apart: 5, of which 2 were waited for; matrix products, arithmetic and copies ran while one was open for 10% of the time, Pallas kernels for 0%

profile of v1, /device:TPU:2, one launch (start us, length us, event | category | flops | bytes accessed | tf_op | source)
XLA Modules:
  0.0 266.7 jit_solution(2806579723638151195)
XLA Ops:
  7.2 0.7 all-gather.5.cloned.1.call-update
  8.0 0.8 select_reduce_fusion
  8.7 1.3 fusion.2
  10.2 44.1 %all_to_all.57 = bf16[128,16,128]{2,1,0:T(8,128)(2,1)S(1)} all-to-all(bf16[128,16,128]{2,1,0:T(8,128)(2,1)S(1)} %bitcast.73), channel_id=1, replica_groups=mesh['dp'=16,'pipe'=4,'tensor'=8] {'dp'}, dimensions={0} | all-to-all | bytes 1048576 | tf_op jit(solution)/shard_map/all_to_all | solution.py:49
  54.3 0.8 copy-done.2
  55.1 1.0 convolution_convert_fusion.4
  56.2 3.2 %convolution_convert_fusion.1 = bf16[1024,2048]{1,0:T(8,128)(2,1)} fusion(bf16[1024,256]{1,0:T(8,128)(2,1)S(1)} %copy-done.1, bf16[256,2048]{1,0:T(8,128)(2,1)S(1)} %copy-done), kind=kOutput, calls=%fused_computation.1 | convolution fusion | flops 1075838976 | bytes 5767168 | tf_op jit(solution)/shard_map/dot_general | solution.py:59
  59.5 2.4 copy.61
  62.0 0.2 dynamic-slice_reduce_fusion
  62.1 0.4 convolution_convert_fusion
  62.5 0.2 reshape.74
  62.7 24.5 %all_to_all.58 = bf16[16,4,2048]{2,1,0:T(4,128)(2,1)S(1)} all-to-all(bf16[16,4,2048]{2,1,0:T(4,128)(2,1)S(1)} %reshape.74), channel_id=1, replica_groups=mesh['dp'=16,'pipe'=4,'tensor'=8] {'dp'}, dimensions={0} | all-to-all | bytes 524288 | tf_op jit(solution)/shard_map/all_to_all | solution.py:50
  87.6 0.4 copy-done.4
  88.1 24.9 %all_gather.12 = bf16[1024,128]{1,0:T(8,128)(2,1)S(1)} all-gather(bf16[32,128]{1,0:T(8,128)(2,1)S(1)} %pad_maximum_fusion), channel_id=1, replica_groups=mesh['dp'=16,'pipe'=4,'tensor'=8] {'pipe','tensor'}, dimensions={0}, use_global_device_ids=true | all-gather | bytes 270336 | tf_op jit(solution)/shard_map/all_gather | solution.py:98
  113.0 0.3 fusion.1
  113.3 1.1 copy.41
  114.4 5.8 %all-to-all-start.2 = ((bf16[8,256,128]{2,0,1:T(8,128)(2,1)}), bf16[8,256,128]{2,0,1:T(8,128)(2,1)S(1)}, u32[]{:S(2)}, u32[]{:S(2)}) async-start(bf16[8,256,128]{2,0,1:T(8,128)(2,1)} %copy.41), calls=%async_computation.3 | async-start | bytes 1048576 | tf_op jit(solution)/shard_map/all_to_all | solution.py:122
  120.2 0.3 fusion.28
  120.5 29.0 %all-to-all-done.2 = bf16[8,256,128]{2,0,1:T(8,128)(2,1)S(1)} async-done(((bf16[8,256,128]{2,0,1:T(8,128)(2,1)}), bf16[8,256,128]{2,0,1:T(8,128)(2,1)S(1)}, u32[]{:S(2)}, u32[]{:S(2)}) %all-to-all-start.2) | async-done | bytes 524320 | tf_op jit(solution)/shard_map/all_to_all | solution.py:122
  149.5 0.3 copy.44
  149.8 0.3 fusion.19
  150.1 1.3 copy.52
  151.5 1.1 constant_dynamic-slice_fusion
  152.5 4.3 %fusion = bf16[1024,256]{1,0:T(8,128)(2,1)} fusion(f32[1024,256]{1,0:T(8,128)S(1)} %bitcast.76, bf16[1024,2048]{1,0:T(8,128)(2,1)} %all-gather.5.cloned.1.call-done, bf16[256,2048]{1,0:T(8,128)(2,1)S(1)} %copy-done), kind=kOutput, calls=%fused_computation.4 | convolution fusion | flops 1074266112 | bytes 6815744 | tf_op jit(solution)/shard_map/dot_general | solution.py:101
  156.8 4.8 %reduce_sum.22 = bf16[1024,128]{1,0:T(8,128)(2,1)S(1)} reduce(bf16[32,1024,128]{2,1,0:T(8,128)(2,1)} %all-gather.3.cloned.1.call-done, bf16[]{:T(256)} %constant.38.clone.1), dimensions={0}, to_apply=%region_2.3 | reduce | flops 4063232 | bytes 8650754 | tf_op jit(solution)/shard_map/reduce_sum | solution.py:57
  161.8 0.2 convolution_convert_fusion.5
  162.1 0.8 reshape.83
  162.9 6.6 %all-to-all-start.3 = ((bf16[16,2,1024]{2,1,0:T(2,128)(2,1)}), bf16[16,2,1024]{2,1,0:T(2,128)(2,1)S(1)}, u32[]{:S(2)}, u32[]{:S(2)}) async-start(bf16[16,2,1024]{2,1,0:T(2,128)(2,1)} %reshape.83), calls=%async_computation.4 | async-start | bytes 131072 | tf_op jit(solution)/shard_map/all_to_all | solution.py:125
  169.6 0.2 fusion.9
  169.8 87.5 %reduce-scatter.2.cloned.1.call-done = bf16[32,2048]{1,0:T(8,128)(2,1)} async-done(((bf16[1024,2048]{1,0:T(8,128)(2,1)}), bf16[32,2048]{1,0:T(8,128)(2,1)}) %reduce-scatter.2.cloned.1.call-update) | async-done | bytes 131088 | tf_op jit(solution)/shard_map/reduce_scatter | solution.py:58
  257.3 1.6 fusion.7
  259.4 0.8 fusion.17
  (34 shorter events, 1.7 us)
Async XLA Ops:
  7.2 49.0 %copy-start = (bf16[256,2048]{1,0:T(8,128)(2,1)S(1)}, bf16[256,2048]{1,0:T(8,128)(2,1)}, u32[]{:S(2)}) copy-start(bf16[256,2048]{1,0:T(8,128)(2,1)} %param.8) | copy-start | bytes 3145732
  7.2 47.9 %copy-start.1 = (bf16[1024,256]{1,0:T(8,128)(2,1)S(1)}, bf16[1024,256]{1,0:T(8,128)(2,1)}, u32[]{:S(2)}) copy-start(bf16[1024,256]{1,0:T(8,128)(2,1)} %param.7) | copy-start | bytes 1572868
  7.2 144.3 %all-gather.5.cloned.1.call-start = ((), (), s32[]{:S(2)}) async-start(), calls=%async_computation.7 | async-start | bytes 4325376 | tf_op jit(solution)/shard_map/all_gather | solution.py:97
  7.9 148.9 %all-gather.3.cloned.1.call-start = ((), (), s32[]{:S(2)}) async-start(), calls=%async_computation.6 | async-start | bytes 8650752 | tf_op jit(solution)/shard_map/all_gather | solution.py:57
  54.3 0.8 copy-start.2
  56.1 201.2 %reduce-scatter.2.cloned.1.call-start = ((), (), s32[]{:S(2)}) async-start(), calls=%async_computation.5 | async-start | bytes 4325376 | tf_op jit(solution)/shard_map/reduce_scatter | solution.py:58
  59.4 27.9 %copy-start.6 = (bf16[32,2048]{1,0:T(8,128)(2,1)S(1)}, bf16[32,2048]{1,0:T(8,128)(2,1)}, u32[]{:S(2)}) copy-start(bf16[32,2048]{1,0:T(8,128)(2,1)} %param.13) | copy-start | bytes 393220
  62.5 57.7 %copy-start.3 = (bf16[16,8,16,128]{3,2,0,1:T(8,128)(2,1)S(1)}, bf16[16,8,16,128]{3,2,0,1:T(8,128)(2,1)}, u32[]{:S(2)}) copy-start(bf16[16,8,16,128]{3,2,0,1:T(8,128)(2,1)} %copy-done.2) | copy-start | bytes 1572868
  87.3 0.7 copy-start.4
  114.4 35.1 %all-to-all-start.2 = ((bf16[8,256,128]{2,0,1:T(8,128)(2,1)}), bf16[8,256,128]{2,0,1:T(8,128)(2,1)S(1)}, u32[]{:S(2)}, u32[]{:S(2)}) async-start(bf16[8,256,128]{2,0,1:T(8,128)(2,1)} %copy.41), calls=%async_computation.3 | async-start | bytes 1048576 | tf_op jit(solution)/shard_map/all_to_all | solution.py:122
  156.8 12.7 %copy-start.5 = (bf16[64,2048]{1,0:T(8,128)(2,1)S(1)}, bf16[64,2048]{1,0:T(8,128)(2,1)}, u32[]{:S(2)}) copy-start(bf16[64,2048]{1,0:T(8,128)(2,1)} %copy-done.4) | copy-start | bytes 786436
  162.9 96.0 %all-to-all-start.3 = ((bf16[16,2,1024]{2,1,0:T(2,128)(2,1)}), bf16[16,2,1024]{2,1,0:T(2,128)(2,1)S(1)}, u32[]{:S(2)}, u32[]{:S(2)}) async-start(bf16[16,2,1024]{2,1,0:T(2,128)(2,1)} %reshape.83), calls=%async_computation.4 | async-start | bytes 131072 | tf_op jit(solution)/shard_map/all_to_all | solution.py:125
Sparse Core Ops, SparseCore 0:
  11.1 65.4 all-gather.4
  79.8 68.0 all-gather.2
  152.4 104.8 reduce-scatter.1
